TPU v7x, 128 devices: a whole 4x4x4 slice. The times are simulated.
128 devices in a mesh: seq: 16 (over z_lo, y, core), head: 8 (over z_hi, x).
Axes of the slice: x: 4, y: 4, z: 4 (z_hi: 2, z_lo: 2; z = z_hi * 2 + z_lo), core: 2. Of those that a mesh axis runs over, the one named last changes fastest.
Arguments:
- queries: bfloat16 [8192, 4096], P('seq', 'head'), may hold values from -6 to 6
- new_keys: bfloat16 [8192, 4096], P('seq', 'head'), may hold values from -6 to 6
- new_values: bfloat16 [8192, 4096], P('seq', 'head'), may hold values from -6 to 6
- pool_keys: bfloat16 [16384, 4096], P('seq', 'head'), may hold values from -6 to 6
- pool_values: bfloat16 [16384, 4096], P('seq', 'head'), may hold values from -6 to 6
- cache_len: int32 [4], replicated, may hold values from 128 to 4096, as said below
- cached_table: int32 [4, 32], replicated, may hold values from -1 to 127, as said below
- free_blocks: int32 [4, 16], replicated, may hold values from 0 to 127, as said below
- residual_in: bfloat16 [8192, 7168], P('seq', 'head'), may hold values from -26 to 26
- out_weight: bfloat16 [4096, 7168], P('head'), may hold values from -2.390625 to 2.390625
- out_bias: float32 [7168], P('head'), may hold values from -3 to 3
- ln_gain: float32 [7168], P('head'), may hold values from 0.1 to 1.9
- ln_bias: float32 [7168], P('head'), may hold values from -3 to 3
Outputs:
- hidden: bfloat16 [8192, 7168], P('seq', 'head')
- normed: bfloat16 [8192, 7168], P('seq', 'head')
- keys_out: bfloat16 [16384, 4096], P('seq', 'head')
- values_out: bfloat16 [16384, 4096], P('seq', 'head')
Inputs may be any that keep to these rules, and one draw needn't show every extreme that they name: `cache_len`: a multiple of 128; exactly one prompt has 4096 cached positions. `cached_table`: entry [p, j] names the pool block that holds cached positions j * 128 to j * 128 + 127 of prompt p when j < cache_len[p] / 128, and is -1 otherwise; the named blocks are all different and lie anywhere in the pool. `free_blocks`: all different and never named by cached_table; block free_blocks[p, j] lies in the pool rows held by the same index of seq as token row p * 2048 + j * 128, that is free_blocks[p, j] * 128 // 1024 == (p * 2048 + j * 128) // 512.
All inputs are finite; a program needn't handle non-finite values.
Results may differ from a plain program's by a relative error of at most 0.022.
Values may be sent and summed in bfloat16 or wider, within the bound.
No kernel may reach another device: no remote copies, remote signals or barrier semaphores. Data moves between devices by JAX's collectives and lax.ppermute only.
A program may use at most 384 MiB of HBM per device.

v0:
```python
import jax
import jax.numpy as jnp
from jax import lax
from jax.sharding import PartitionSpec as P

D = 7168
HD = 128
NEW_LEN = 2048
BLOCK = 128
NEGATIVE = -1e30


def key_facts(block_count, cached_table, free_blocks, cache_len):
    block_ids = jnp.arange(block_count, dtype=jnp.int32)
    prompt_count, cached_count = cached_table.shape
    fresh_count = free_blocks.shape[1]
    prompt_ids = jnp.arange(prompt_count, dtype=jnp.int32)
    in_cache = cached_table[None, :, :] == block_ids[:, None, None]
    in_fresh = free_blocks[None, :, :] == block_ids[:, None, None]
    owner = jnp.sum(jnp.where(in_cache, prompt_ids[None, :, None] + 1, 0), axis=(1, 2))
    owner = owner + jnp.sum(jnp.where(in_fresh, prompt_ids[None, :, None] + 1, 0), axis=(1, 2)) - 1
    cached_slot = jnp.arange(cached_count, dtype=jnp.int32)
    fresh_slot = (cache_len // BLOCK)[:, None] + jnp.arange(fresh_count, dtype=jnp.int32)[None, :]
    logical = jnp.sum(jnp.where(in_cache, cached_slot[None, None, :], 0), axis=(1, 2))
    logical = logical + jnp.sum(jnp.where(in_fresh, fresh_slot[None, :, :], 0), axis=(1, 2))
    key_owner = jnp.repeat(owner, BLOCK)
    key_place = (logical[:, None] * BLOCK + jnp.arange(BLOCK, dtype=jnp.int32)[None, :]).reshape(-1)
    return (key_owner, key_place)


def query_facts(first_row, row_count, cache_len):
    rows = first_row + jnp.arange(row_count, dtype=jnp.int32)
    owner = rows // NEW_LEN
    place = rows % NEW_LEN
    prompt_ids = jnp.arange(cache_len.shape[0], dtype=jnp.int32)
    limit = (
        jnp.sum(jnp.where(owner[:, None] == prompt_ids[None, :], cache_len[None, :], 0), axis=1)
        + place
    )
    return (owner, limit)


def attend(query_rows, query_owner, query_limit, keys, values, key_owner, key_place):
    row_count = query_rows.shape[0]
    heads_here = query_rows.shape[1] // HD
    key_count = keys.shape[0]
    query_split = query_rows.reshape(row_count, heads_here, HD)
    key_split = keys.reshape(key_count, heads_here, HD)
    value_split = values.reshape(key_count, heads_here, HD)
    visible = (key_owner[None, :] == query_owner[:, None]) & (
        key_place[None, :] <= query_limit[:, None]
    )
    scores = jnp.einsum(
        "rhd,khd->hrk", query_split, key_split, preferred_element_type=jnp.float32
    ) * HD ** (-0.5)
    scores = jnp.where(visible[None, :, :], scores, NEGATIVE)
    peak = jnp.max(scores, axis=2)
    weights = jnp.where(visible[None, :, :], jnp.exp(scores - peak[:, :, None]), 0.0)
    total = jnp.sum(weights, axis=2)
    mixed = jnp.einsum(
        "hrk,khd->rhd",
        weights.astype(jnp.bfloat16),
        value_split,
        preferred_element_type=jnp.float32,
    )
    return (peak.T, total.T, mixed.reshape(row_count, heads_here * HD))


def combine(first, second):
    peak = jnp.maximum(first[0], second[0])
    scale_first = jnp.exp(first[0] - peak)
    scale_second = jnp.exp(second[0] - peak)
    total = second[1] * scale_second
    row_count, heads_here = peak.shape
    mixed = first[2].reshape(row_count, heads_here, HD) * scale_first[:, :, None]
    mixed = second[2].reshape(row_count, heads_here, HD) * scale_second[:, :, None]
    return (peak, total, mixed.reshape(row_count, heads_here * HD))


def shards(
    queries,
    new_keys,
    new_values,
    pool_keys,
    pool_values,
    cache_len,
    cached_table,
    free_blocks,
    residual_in,
    out_weight,
    out_bias,
    ln_gain,
    ln_bias,
):
    token_rows, width = queries.shape
    heads_here = width // HD
    pool_rows = pool_keys.shape[0]
    per_device = pool_rows // BLOCK
    fresh_device = token_rows // BLOCK
    position = lax.axis_index("seq")
    first_row = position * token_rows
    prompt_here = first_row // NEW_LEN
    first_slot = first_row % NEW_LEN // BLOCK
    targets = (
        lax.dynamic_slice(free_blocks, (prompt_here, first_slot), (1, fresh_device))[0]
        - position * per_device
    )
    keys_out = (
        pool_keys.reshape(per_device, BLOCK, width)
        .at[targets]
        .set(new_keys.reshape(fresh_device, BLOCK, width))
        .reshape(pool_rows, width)
    )
    values_out = (
        pool_values.reshape(per_device, BLOCK, width)
        .at[targets]
        .set(new_values.reshape(fresh_device, BLOCK, width))
        .reshape(pool_rows, width)
    )
    own_owner, own_limit = query_facts(first_row, token_rows, cache_len)
    start_state = (
        jnp.full((token_rows, heads_here), NEGATIVE, jnp.float32),
        jnp.zeros((token_rows, heads_here), jnp.float32),
        jnp.zeros((token_rows, width), jnp.float32),
    )
    piece_keys = lax.all_gather(keys_out, "seq", axis=0, tiled=True)
    piece_values = lax.all_gather(values_out, "seq", axis=0, tiled=True)
    key_owner, key_place = key_facts(
        piece_keys.shape[0] // BLOCK, cached_table, free_blocks, cache_len
    )
    peak, total, mixed = combine(
        start_state,
        attend(queries, own_owner, own_limit, piece_keys, piece_values, key_owner, key_place),
    )
    attn = (
        (mixed.reshape(token_rows, heads_here, HD) / total[:, :, None])
        .reshape(token_rows, width)
        .astype(jnp.bfloat16)
    )
    projected = jnp.dot(attn, out_weight, preferred_element_type=jnp.float32)
    summed = lax.psum_scatter(
        projected.astype(jnp.bfloat16), "head", scatter_dimension=1, tiled=True
    ).astype(jnp.float32)
    stream = residual_in.astype(jnp.float32) + summed + out_bias[None, :]
    mean = lax.psum(jnp.sum(stream, axis=1), "head") / D
    centred = stream - mean[:, None]
    variance = lax.psum(jnp.sum(centred * centred, axis=1), "head") / D
    normed = (
        centred * lax.rsqrt(variance[:, None] + 1e-05) * ln_gain[None, :] + ln_bias[None, :]
    ).astype(jnp.bfloat16)
    return (stream.astype(jnp.bfloat16), normed, keys_out, values_out)


def solution(mesh):
    in_specs = (
        P("seq", "head"),
        P("seq", "head"),
        P("seq", "head"),
        P("seq", "head"),
        P("seq", "head"),
        P(),
        P(),
        P(),
        P("seq", "head"),
        P("head", None),
        P("head"),
        P("head"),
        P("head"),
    )
    out_specs = (P("seq", "head"), P("seq", "head"), P("seq", "head"), P("seq", "head"))
    return jax.shard_map(shards, mesh=mesh, in_specs=in_specs, out_specs=out_specs, check_vma=False)
```

profile of v0, /device:TPU:0, one launch (start us, length us, event | category | flops | bytes accessed | tf_op | source)
XLA Modules:
  0.0 465.4 jit_solution(8003422405766926117)
XLA Ops:
  7.2 0.0 copy-start
  7.2 0.0 all-gather.5.cloned.1.call-start
  7.2 1.3 copy.59
  8.5 1.2 copy.60
  9.7 0.8 fusion.22
  10.5 1.7 scatter_fusion.1
  12.2 0.0 copy-start.4
  12.2 1.3 copy.38
  13.5 0.0 all-gather.5.cloned.1.call-update
  13.5 0.0 all-gather.3.cloned.1.call-start
  13.6 1.7 scatter_fusion
  15.3 0.0 copy-start.3
  15.3 1.0 copy-done.3
  16.3 0.0 all-gather.3.cloned.1.call-update
  16.3 0.0 reduce-scatter.4.cloned.1.call-start
  16.4 0.7 select_reduce_fusion.4
  17.1 0.8 select_reduce_fusion.1
  17.9 0.7 and_select_fusion
  18.6 0.1 iota_add_fusion
  18.6 0.8 select_reduce_fusion.3
  19.4 0.1 add_bitcast_fusion
  19.5 0.1 broadcast_bitcast_fusion
  19.6 13.3 %compare_and_fusion = pred[512,16384]{0,1:T(8,128)(4,1)} fusion(s32[512]{0:T(512)S(1)} %fusion.18, s32[512]{0:T(512)S(1)} %add_select_fusion.1, s32[16384]{0:T(1024)S(1)} %add_bitcast_fusion, s32[16384]{0:T(1024)S(1)} %broadcast_bitcast_fusion), kind=kLoop, calls=%fused_computation.9 | loop fusion | flops 25165824 | bytes 8523776 | tf_op jit(solution)/shard_map/and | solution.py:50
  32.9 74.9 %all-gather.5.cloned.1.call-done = bf16[16384,512]{0,1:T(8,128)(2,1)} async-done(((bf16[1024,512]{0,1:T(8,128)(2,1)}), bf16[16384,512]{0,1:T(8,128)(2,1)}) %all-gather.5.cloned.1.call-update) | async-done | bytes 16777232 | tf_op jit(solution)/shard_map/all_gather | solution.py:126
  107.8 0.0 copy-done
  107.8 59.0 %fusion = (f32[4,512]{1,0:T(4,128)S(1)}, f32[4,16384,512]{2,1,0:T(8,128)}) fusion(pred[512,16384]{0,1:T(8,128)(4,1)} %compare_and_fusion, bf16[16384,4,128]{0,2,1:T(8,128)(2,1)} %bitcast.79, bf16[512,512]{1,0:T(8,128)(2,1)S(1)} %copy-done), kind=kOutput, calls=%fused_computation.4 | convolution fusion | flops 8690595840 | bytes 159916032 | tf_op jit(solution)/shard_map/rhd,khd->hrk/dot_general | solution.py:53
  166.8 0.0 copy-done.4
  166.8 45.4 %fusion.1 = f32[4,512]{1,0:T(4,128)S(1)} fusion(f32[4,16384,512]{2,1,0:T(8,128)} %get-tuple-element.17, f32[4,512]{1,0:T(4,128)S(1)} %get-tuple-element.16, pred[512,16384]{0,1:T(8,128)(4,1)} %compare_and_fusion), kind=kLoop, calls=%fused_computation.5 | loop fusion | flops 167770112 | bytes 142622720 | tf_op jit(solution)/shard_map/reduce_sum | solution.py:59
  212.2 0.0 all-gather.3.cloned.1.call-done
  212.2 21.3 %copy.37 = bf16[16384,512]{0,1:T(8,128)(2,1)} copy(bf16[16384,512]{1,0:T(8,128)(2,1)} %all-gather.3.cloned.1.call-done) | data formatting | bytes 33554432 | tf_op jit(solution)/shard_map/all_gather | solution.py:127
  233.5 52.8 %divide_convert_fusion = bf16[512,4,128]{0,2,1:T(8,128)(2,1)S(1)} fusion(f32[512,4]{0,1:T(4,128)S(1)} %get-tuple-element.14, f32[512,4]{0,1:T(4,128)S(1)} %get-tuple-element.15, bf16[16384,4,128]{0,2,1:T(8,128)(2,1)} %bitcast.68, f32[4,16384,512]{2,1,0:T(8,128)} %get-tuple-element.17, f32[4,512]{1,0:T(4,128)S(1)} %get-tuple-element.16, ...), kind=kOutput, calls=%fused_computation.18 | convolution fusion | flops 8758493184 | bytes 159932416 | tf_op jit(solution)/shard_map/hrk,khd->rhd/dot_general | solution.py:60
  286.3 0.0 copy-start.2
  286.3 0.0 copy-start.5
  286.3 0.0 copy-start.1
  286.3 9.5 %convolution_convert_fusion = bf16[512,7168]{1,0:T(8,128)(2,1)} fusion(bf16[512,512]{0,1:T(8,128)(2,1)S(1)} %bitcast.78, bf16[512,7168]{1,0:T(8,128)(2,1)} %param.22), kind=kOutput, calls=%fused_computation.10 | convolution fusion | flops 3761766400 | bytes 15204352 | tf_op jit(solution)/shard_map/dot_general | solution.py:140
  295.9 0.0 copy-start.6
  295.9 0.0 copy-start.7
  295.9 10.4 %copy.44 = bf16[512,7168]{0,1:T(8,128)(2,1)} copy(bf16[512,7168]{1,0:T(8,128)(2,1)} %convolution_convert_fusion) | data formatting | bytes 14680064
  306.3 0.0 reduce-scatter.4.cloned.1.call-update
  306.3 108.4 %reduce-scatter.4.cloned.1.call-done = bf16[896,512]{1,0:T(8,128)(2,1)} async-done(((bf16[7168,512]{1,0:T(8,128)(2,1)}), bf16[896,512]{1,0:T(8,128)(2,1)}) %reduce-scatter.4.cloned.1.call-update) | async-done | bytes 917520
  414.7 1.5 copy.45
  416.3 0.0 copy-done.2
  416.3 0.0 copy-done.5
  416.3 0.4 fusion.12
  416.7 20.3 %psum.14 = f32[512]{0:T(512)S(1)} all-reduce(f32[512]{0:T(512)S(1)} %fusion.12), channel_id=1, replica_groups=mesh['seq'=16,'head'=8] {'head'}, use_global_device_ids=true, to_apply=%region_11.12 | all-reduce | flops 512 | bytes 4096 | tf_op jit(solution)/shard_map/psum | solution.py:145
  437.0 0.5 multiply_reduce_fusion
  437.5 19.6 %psum.15 = f32[512]{0:T(512)S(1)} all-reduce(f32[512]{0:T(512)S(1)} %multiply_reduce_fusion), channel_id=1, replica_groups=mesh['seq'=16,'head'=8] {'head'}, use_global_device_ids=true, to_apply=%region_13.14 | all-reduce | flops 512 | bytes 4096 | tf_op jit(solution)/shard_map/psum | solution.py:147
  457.1 0.0 copy-done.6
  457.1 0.0 copy-done.7
  457.1 1.8 add_convert_fusion
  458.9 0.0 copy-done.1
  (7 shorter events, 0.1 us)
Async XLA Ops:
  7.2 100.6 %copy-start = (bf16[512,512]{1,0:T(8,128)(2,1)S(1)}, bf16[512,512]{1,0:T(8,128)(2,1)}, u32[]{:S(2)}) copy-start(bf16[512,512]{1,0:T(8,128)(2,1)} %param.13) | copy-start | bytes 1572868
  7.2 100.6 %all-gather.5.cloned.1.call-start = ((), (), s32[]{:S(2)}) async-start(), calls=%async_computation.2 | async-start | bytes 17825792 | tf_op jit(solution)/shard_map/all_gather | solution.py:126
  12.2 154.6 %copy-start.4 = (bf16[8,128,512]{2,1,0:T(8,128)(2,1)}, bf16[8,128,512]{2,1,0:T(8,128)(2,1)S(1)}, u32[]{:S(2)}) copy-start(bf16[8,128,512]{2,1,0:T(8,128)(2,1)S(1)} %scatter_fusion.1) | copy-start | bytes 3145732
  13.5 198.6 %all-gather.3.cloned.1.call-start = ((), (), s32[]{:S(2)}) async-start(), calls=%async_computation.1 | async-start | bytes 17825792 | tf_op jit(solution)/shard_map/all_gather | solution.py:127
  15.3 1.0 copy-start.3
  16.3 398.4 %reduce-scatter.4.cloned.1.call-start = ((), (), s32[]{:S(2)}) async-start(), calls=%async_computation.3 | async-start | bytes 8257536
  286.3 130.0 %copy-start.2 = (bf16[512,896]{1,0:T(8,128)(2,1)S(1)}, bf16[512,896]{1,0:T(8,128)(2,1)}, u32[]{:S(2)}) copy-start(bf16[512,896]{1,0:T(8,128)(2,1)} %param.21) | copy-start | bytes 2752516
  286.3 130.0 %copy-start.5 = (f32[896]{0:T(1024)S(1)}, f32[896]{0:T(1024)}, u32[]{:S(2)}) copy-start(f32[896]{0:T(1024)} %param.23) | copy-start | bytes 10756
  286.3 172.6 %copy-start.1 = (bf16[512,512]{1,0:T(8,128)(2,1)S(1)}, bf16[512,512]{1,0:T(8,128)(2,1)}, u32[]{:S(2)}) copy-start(bf16[512,512]{1,0:T(8,128)(2,1)} %param.13) | copy-start | bytes 1572868
  295.9 161.2 %copy-start.6 = (f32[896]{0:T(1024)S(1)}, f32[896]{0:T(1024)}, u32[]{:S(2)}) copy-start(f32[896]{0:T(1024)} %param.25) | copy-start | bytes 10756
  295.9 161.2 %copy-start.7 = (f32[896]{0:T(1024)S(1)}, f32[896]{0:T(1024)}, u32[]{:S(2)}) copy-start(f32[896]{0:T(1024)} %param.24) | copy-start | bytes 10756
Sparse Core Ops, SparseCore 0:
  13.7 94.0 all-gather.4
  110.1 92.4 all-gather.2
  306.5 108.2 reduce-scatter.3
where the time goes:
time: 467 us; the launch traced here: 465 us
  waiting for transfers between devices  183 us (39%)
  matrix products  121 us (26%)
  other arithmetic  65.2 us (14%)
  local copies, waits for them, and re-layouts  41.5 us (9%)
  blocking collectives  39.9 us (9%)
  between operations  13.9 us (3%)
    unnamed x4, waiting for transfers between devices  108 us
    all_gather x1, waiting for transfers between devices, shards(): piece_keys = lax.all_gather(keys_out, 'seq', axis=0, tiled=True)  74.9 us
    dot_general x1, matrix products, attend(): jnp.einsum('rhd,khd->hrk', query_split, key_split, preferred_element_type...  59 us
    dot_general x1, matrix products, attend(): jnp.einsum('hrk,khd->rhd', weights.astype(jnp.bfloat16), value_split, pre...  52.8 us
    reduce_sum x1, other arithmetic, attend(): total = jnp.sum(weights, axis=2)  45.4 us
    all_gather x1, local copies, waits for them, and re-layouts, shards(): piece_values = lax.all_gather(values_out, 'seq', axis=0, tiled=True)  21.3 us
    psum x1, blocking collectives, shards(): mean = lax.psum(jnp.sum(stream, axis=1), 'head') / D  20.3 us
    psum x1, blocking collectives, shards(): variance = lax.psum(jnp.sum(centred * centred, axis=1), 'head') / D  19.6 us
  transfers between devices with their start and end apart: 3, of which 2 were waited for; matrix products, arithmetic and copies ran while one was open for 26% of the time, Pallas kernels for 0%

commit v1 on v0

--- a/solution.py
+++ b/solution.py
@@ -123,7 +123,10 @@
         jnp.zeros((token_rows, heads_here), jnp.float32),
         jnp.zeros((token_rows, width), jnp.float32),
     )
-    piece_keys = lax.all_gather(keys_out, "seq", axis=0, tiled=True)
+    peers = lax.axis_size("seq")
+    shards_2 = jnp.stack([keys_out for _ in range(peers)])
+    shards_2 = lax.all_to_all(shards_2, "seq", split_axis=0, concat_axis=0)
+    piece_keys = jnp.concatenate(shards_2, axis=0)
     piece_values = lax.all_gather(values_out, "seq", axis=0, tiled=True)
     key_owner, key_place = key_facts(
         piece_keys.shape[0] // BLOCK, cached_table, free_blocks, cache_len

time: 467 us -> 711 us (1.52)
  waiting for transfers between devices: 183 us -> 381 us
  local copies, waits for them, and re-layouts: 41.5 us -> 89 us
    all_to_all x0 -> x1, waiting for transfers between devices: none -> 271 us  [shards(): shards_2 = lax.all_to_all(shards_2, 'seq', split_axis=0, concat_axis=0)]
    all_gather x1 -> x0, waiting for transfers between devices: 74.9 us -> none  [shards(): piece_keys = lax.all_gather(keys_out, 'seq', axis=0, tiled=True)]
    another operation x0 -> x3, local copies, waits for them, and re-layouts: none -> 32.3 us  [the longest x1 25.6 us: attend(): key_split = keys.reshape(key_count, heads_here, HD)]
    all_to_all x0 -> x1, local copies, waits for them, and re-layouts: none -> 18.7 us  [shards(): shards_2 = lax.all_to_all(shards_2, 'seq', split_axis=0, concat_axis=0)]
    unnamed x20 -> x29, local copies, waits for them, and re-layouts: 15.5 us -> 14.3 us
    unnamed x4 -> x3, waiting for transfers between devices: 108 us -> 110 us
  transfers between devices with their start and end apart: 3 -> 3, of which waited for: 2 -> 2; matrix products, arithmetic and copies ran while one was open for 26% -> 22% of each run, Pallas kernels for 0% -> 0%
where the time goes in v1:
time: 711 us; the launch traced here: 709 us
  waiting for transfers between devices  381 us (54%)
  matrix products  118 us (17%)
  local copies, waits for them, and re-layouts  89 us (13%)
  other arithmetic  61 us (9%)
  blocking collectives  39.9 us (6%)
  between operations  14.3 us (2%)
    all_to_all x1, waiting for transfers between devices, shards(): shards_2 = lax.all_to_all(shards_2, 'seq', split_axis=0, concat_axis=0)  271 us
    unnamed x3, waiting for transfers between devices  110 us
    dot_general x1, matrix products, attend(): jnp.einsum('rhd,khd->hrk', query_split, key_split, preferred_element_type...  55.8 us
    dot_general x1, matrix products, attend(): jnp.einsum('hrk,khd->rhd', weights.astype(jnp.bfloat16), value_split, pre...  52.8 us
    reduce_sum x1, other arithmetic, attend(): total = jnp.sum(weights, axis=2)  43.7 us
    another operation x1, local copies, waits for them, and re-layouts, attend(): key_split = keys.reshape(key_count, heads_here, HD)  25.6 us
    all_gather x1, local copies, waits for them, and re-layouts, shards(): piece_values = lax.all_gather(values_out, 'seq', axis=0, tiled=True)  21.3 us
    psum x1, blocking collectives, shards(): mean = lax.psum(jnp.sum(stream, axis=1), 'head') / D  20.3 us
  transfers between devices with their start and end apart: 3, of which 2 were waited for; matrix products, arithmetic and copies ran while one was open for 22% of the time, Pallas kernels for 0%

profile of v1, /device:TPU:0, one launch (start us, length us, event | category | flops | bytes accessed | tf_op | source)
XLA Modules:
  0.0 708.9 jit_solution(4044138878841472793)
XLA Ops:
  7.2 0.0 copy-start
  7.2 1.3 copy.54
  8.5 0.8 fusion.22
  9.2 1.7 scatter_fusion.1
  10.9 0.0 copy-start.5
  10.9 0.5 copy.32
  11.5 6.1 stack.3
  17.6 0.0 copy-start.4
  17.6 0.0 copy-start.6
  17.6 0.0 copy-start.12
  17.6 0.0 copy-start.11
  17.6 0.0 copy-start.10
  17.6 0.0 copy-done.5
  17.7 6.2 all-to-all-start
  23.9 0.0 all-gather.2.cloned.1.call-start
  23.9 0.0 copy-done.4
  23.9 0.0 copy-done.6
  23.9 0.7 scatter_fusion
  24.6 0.0 copy-start.3
  24.6 1.0 copy-done.3
  25.6 0.0 all-gather.2.cloned.1.call-update
  25.6 0.0 reduce-scatter.4.cloned.1.call-start
  25.7 0.0 copy-done.12
  25.7 0.1 select_reduce_fusion.4
  25.8 0.0 copy-done.11
  25.8 0.1 select_reduce_fusion.1
  25.9 0.1 iota_add_fusion
  26.0 0.0 copy-done.10
  26.0 0.1 select_reduce_fusion.3
  26.1 0.1 add_bitcast_fusion
  26.2 0.1 broadcast_bitcast_fusion
  26.3 13.3 %compare_and_fusion = pred[512,16384]{0,1:T(8,128)(4,1)} fusion(s32[512]{0:T(512)S(1)} %fusion.18, s32[512]{0:T(512)S(1)} %add_select_fusion.1, s32[16384]{0:T(1024)S(1)} %add_bitcast_fusion, s32[16384]{0:T(1024)S(1)} %broadcast_bitcast_fusion), kind=kLoop, calls=%fused_computation.9 | loop fusion | flops 25165824 | bytes 8523776 | tf_op jit(solution)/shard_map/and | solution.py:50
  39.6 270.9 %all-to-all-done = bf16[16,1024,512]{1,2,0:T(8,128)(2,1)} async-done(((bf16[16,1024,512]{1,2,0:T(8,128)(2,1)}), bf16[16,1024,512]{1,2,0:T(8,128)(2,1)}, u32[]{:S(2)}, u32[]{:S(2)}) %all-to-all-start) | async-done | bytes 16777248 | tf_op jit(solution)/shard_map/all_to_all | solution.py:128
  310.5 18.7 %copy.33 = bf16[16,1024,512]{1,0,2:T(8,128)(2,1)} copy(bf16[16,1024,512]{1,2,0:T(8,128)(2,1)} %all-to-all-done) | data formatting | bytes 33554432 | tf_op jit(solution)/shard_map/all_to_all | solution.py:128
  329.2 25.6 %reshape_reshape.3 = bf16[16384,4,128]{0,2,1:T(8,128)(2,1)} reshape(bf16[16,1024,512]{1,0,2:T(8,128)(2,1)} %copy.33) | data formatting | bytes 33554432 | tf_op jit(solution)/shard_map/reshape;reshape | solution.py:48
  354.8 0.0 copy-done
  354.8 55.8 %fusion = (f32[4,512]{1,0:T(4,128)S(1)}, f32[4,16384,512]{2,1,0:T(8,128)}) fusion(pred[512,16384]{0,1:T(8,128)(4,1)} %compare_and_fusion, bf16[16384,4,128]{0,2,1:T(8,128)(2,1)} %reshape_reshape.3, bf16[512,512]{1,0:T(8,128)(2,1)S(1)} %copy-done), kind=kOutput, calls=%fused_computation.4 | convolution fusion | flops 8690595840 | bytes 159916032 | tf_op jit(solution)/shard_map/rhd,khd->hrk/dot_general | solution.py:53
  410.6 43.7 %fusion.1 = f32[4,512]{1,0:T(4,128)S(1)} fusion(f32[4,16384,512]{2,1,0:T(8,128)} %get-tuple-element.13, f32[4,512]{1,0:T(4,128)S(1)} %get-tuple-element.12, pred[512,16384]{0,1:T(8,128)(4,1)} %compare_and_fusion), kind=kLoop, calls=%fused_computation.5 | loop fusion | flops 167770112 | bytes 142622720 | tf_op jit(solution)/shard_map/reduce_sum | solution.py:59
  454.4 0.0 all-gather.2.cloned.1.call-done
  454.4 21.3 %copy.31 = bf16[16384,512]{0,1:T(8,128)(2,1)} copy(bf16[16384,512]{1,0:T(8,128)(2,1)} %all-gather.2.cloned.1.call-done) | data formatting | bytes 33554432 | tf_op jit(solution)/shard_map/all_gather | solution.py:130
  475.7 52.8 %divide_convert_fusion = bf16[512,4,128]{0,2,1:T(8,128)(2,1)S(1)} fusion(f32[512,4]{0,1:T(4,128)S(1)} %get-tuple-element.10, f32[512,4]{0,1:T(4,128)S(1)} %get-tuple-element.11, bf16[16384,4,128]{0,2,1:T(8,128)(2,1)} %bitcast.69, f32[4,16384,512]{2,1,0:T(8,128)} %get-tuple-element.13, f32[4,512]{1,0:T(4,128)S(1)} %get-tuple-element.12, ...), kind=kOutput, calls=%fused_computation.18 | convolution fusion | flops 8758493184 | bytes 159932416 | tf_op jit(solution)/shard_map/hrk,khd->rhd/dot_general | solution.py:60
  528.5 0.0 copy-start.2
  528.5 0.0 copy-start.7
  528.5 0.0 copy-start.1
  528.5 9.3 %convolution_convert_fusion = bf16[512,7168]{1,0:T(8,128)(2,1)} fusion(bf16[512,512]{0,1:T(8,128)(2,1)S(1)} %bitcast.79, bf16[512,7168]{1,0:T(8,128)(2,1)} %param.22), kind=kOutput, calls=%fused_computation.10 | convolution fusion | flops 3761766400 | bytes 15204352 | tf_op jit(solution)/shard_map/dot_general | solution.py:143
  537.9 0.0 copy-start.8
  537.9 0.0 copy-start.9
  537.9 10.4 %copy.39 = bf16[512,7168]{0,1:T(8,128)(2,1)} copy(bf16[512,7168]{1,0:T(8,128)(2,1)} %convolution_convert_fusion) | data formatting | bytes 14680064
  548.3 0.0 reduce-scatter.4.cloned.1.call-update
  548.3 109.6 %reduce-scatter.4.cloned.1.call-done = bf16[896,512]{1,0:T(8,128)(2,1)} async-done(((bf16[7168,512]{1,0:T(8,128)(2,1)}), bf16[896,512]{1,0:T(8,128)(2,1)}) %reduce-scatter.4.cloned.1.call-update) | async-done | bytes 917520
  657.9 1.5 copy.40
  659.4 0.0 copy-done.2
  659.5 0.0 copy-done.7
  659.5 0.4 fusion.12
  659.8 20.3 %psum.14 = f32[512]{0:T(512)S(1)} all-reduce(f32[512]{0:T(512)S(1)} %fusion.12), channel_id=1, replica_groups=mesh['seq'=16,'head'=8] {'head'}, use_global_device_ids=true, to_apply=%region_11.12 | all-reduce | flops 512 | bytes 4096 | tf_op jit(solution)/shard_map/psum | solution.py:148
  680.2 0.5 multiply_reduce_fusion
  680.7 19.6 %psum.15 = f32[512]{0:T(512)S(1)} all-reduce(f32[512]{0:T(512)S(1)} %multiply_reduce_fusion), channel_id=1, replica_groups=mesh['seq'=16,'head'=8] {'head'}, use_global_device_ids=true, to_apply=%region_13.14 | all-reduce | flops 512 | bytes 4096 | tf_op jit(solution)/shard_map/psum | solution.py:150
  700.3 0.0 copy-done.8
  700.3 0.0 copy-done.9
  700.3 1.8 add_convert_fusion
  702.1 0.0 copy-done.1
  (8 shorter events, 0.1 us)
Async XLA Ops:
  7.2 347.6 %copy-start = (bf16[512,512]{1,0:T(8,128)(2,1)S(1)}, bf16[512,512]{1,0:T(8,128)(2,1)}, u32[]{:S(2)}) copy-start(bf16[512,512]{1,0:T(8,128)(2,1)} %param.13) | copy-start | bytes 1572868
  10.9 6.7 copy-start.5
  17.6 6.3 copy-start.4
  17.6 6.3 copy-start.6
  17.6 8.1 %copy-start.12 = (s32[4]{0:T(128)S(1)}, s32[4]{0:T(128)}, u32[]{:S(2)}) copy-start(s32[4]{0:T(128)} %param.18) | copy-start | bytes 52
  17.6 8.2 %copy-start.11 = (s32[4,32]{1,0:T(4,128)S(1)}, s32[4,32]{1,0:T(4,128)}, u32[]{:S(2)}) copy-start(s32[4,32]{1,0:T(4,128)} %param.19) | copy-start | bytes 1540
  17.6 8.4 %copy-start.10 = (s32[4,16]{1,0:T(4,128)S(1)}, s32[4,16]{1,0:T(4,128)}, u32[]{:S(2)}) copy-start(s32[4,16]{1,0:T(4,128)} %param.20) | copy-start | bytes 772
  17.7 292.9 %all-to-all-start = ((bf16[16,1024,512]{1,2,0:T(8,128)(2,1)}), bf16[16,1024,512]{1,2,0:T(8,128)(2,1)}, u32[]{:S(2)}, u32[]{:S(2)}) async-start(bf16[16,1024,512]{1,2,0:T(8,128)(2,1)} %stack.3), calls=%async_computation | async-start | bytes 33554432 | tf_op jit(solution)/shard_map/all_to_all | solution.py:128
  23.9 430.5 %all-gather.2.cloned.1.call-start = ((), (), s32[]{:S(2)}) async-start(), calls=%async_computation.2 | async-start | bytes 17825792 | tf_op jit(solution)/shard_map/all_gather | solution.py:130
  24.6 1.0 copy-start.3
  25.6 632.3 %reduce-scatter.4.cloned.1.call-start = ((), (), s32[]{:S(2)}) async-start(), calls=%async_computation.3 | async-start | bytes 8257536
  528.5 131.0 %copy-start.2 = (bf16[512,896]{1,0:T(8,128)(2,1)S(1)}, bf16[512,896]{1,0:T(8,128)(2,1)}, u32[]{:S(2)}) copy-start(bf16[512,896]{1,0:T(8,128)(2,1)} %param.21) | copy-start | bytes 2752516
  528.5 131.0 %copy-start.7 = (f32[896]{0:T(1024)S(1)}, f32[896]{0:T(1024)}, u32[]{:S(2)}) copy-start(f32[896]{0:T(1024)} %param.23) | copy-start | bytes 10756
  528.5 173.6 %copy-start.1 = (bf16[512,512]{1,0:T(8,128)(2,1)S(1)}, bf16[512,512]{1,0:T(8,128)(2,1)}, u32[]{:S(2)}) copy-start(bf16[512,512]{1,0:T(8,128)(2,1)} %param.13) | copy-start | bytes 1572868
  537.9 162.4 %copy-start.8 = (f32[896]{0:T(1024)S(1)}, f32[896]{0:T(1024)}, u32[]{:S(2)}) copy-start(f32[896]{0:T(1024)} %param.25) | copy-start | bytes 10756
  537.9 162.4 %copy-start.9 = (f32[896]{0:T(1024)S(1)}, f32[896]{0:T(1024)}, u32[]{:S(2)}) copy-start(f32[896]{0:T(1024)} %param.24) | copy-start | bytes 10756
Sparse Core Ops, SparseCore 0:
  27.0 279.2 all-gather.1
  548.5 109.3 reduce-scatter.3
